TPU v7x, 256 devices: a whole 4x4x8 slice. The times are simulated.
256 devices in a mesh: dp: 2 (over core), row: 16 (over y, x), col: 8 (over z).
Axes of the slice: x: 4, y: 4, z: 8, core: 2. Of those that a mesh axis runs over, the one named last changes fastest.
Arguments:
- states: bfloat16 [12288, 4096], P(('dp', 'row'), 'col'), may hold values from -6 to 6
- actions: bfloat16 [12288, 24], P(('dp', 'row')), may hold values from -6 to 6
- rewards: float32 [12288], P(('dp', 'row')), may hold values from -6 to 6
- terminal: int32 [12288], P(('dp', 'row')), may hold values 0 or 1
- next_index: int32 [12288], P(('dp', 'row')), may hold values from 0 to 12287
- hidden_weights: bfloat16 [4, 4096, 4096], P(None, 'col', 'row'), may hold values from -0.09375 to 0.09375
- action_weights: bfloat16 [2, 24, 4096], replicated, may hold values from -1.25 to 1.25
- heads: bfloat16 [4096, 27], replicated, may hold values from -0.09375 to 0.09375
- policy_scale: float32 [24], replicated, may hold values from 0.5 to 2
Outputs:
- advantage: float32 [12288], P(('dp', 'row'))
- losses: float32 [3], replicated
- head_grads: float32 [4096, 27], replicated
Inputs may be any that keep to these rules, and one draw needn't show every extreme that they name: `next_index`: any batch row, from any device.
All inputs are finite; a program needn't handle non-finite values. No bound on the sum of `terminal` on one device may be relied on, other than what follows from the above.
Results may differ from a plain program's by a relative error of at most 0.0038.
Values may be sent and summed in bfloat16 or wider, within the bound.
A program may use at most 128 MiB of HBM per device.

v0:
```python
import math
import jax
import jax.numpy as jnp
from jax import lax
from jax.sharding import PartitionSpec as P

D = 4096
GAMMA = 0.99
TAU = 0.7
FLOOR = 0.01


def from_everyone(value, axis):
    copies = jnp.broadcast_to(value, (lax.axis_size(axis), *value.shape))
    return lax.all_to_all(copies, axis, split_axis=0, concat_axis=0, tiled=True)


def of_everyone(value, axis):
    return from_everyone(value, axis).sum(axis=0)


def packed_total(arrays, axis):
    vector, at, done = (jnp.concatenate([a.reshape(-1) for a in arrays]), 0, [])
    subtotal = of_everyone(vector, axis)
    for a in arrays:
        done.append(subtotal[at : at + a.size].reshape(a.shape))
        at += a.size
    return tuple(done)


def in_order(blocks, dim):
    lengths = list(blocks.shape[1:])
    lengths[dim] *= blocks.shape[0]
    return jnp.moveaxis(blocks, 0, dim).reshape(lengths)


def collect(value, axis, dim):
    return in_order(from_everyone(value, axis), dim)


def over_copies(value, axis):
    everything = from_everyone(value, axis)
    return jnp.max(everything, axis=0)


def head_parts(hidden, head_rows):
    first_part = jnp.dot(hidden[0], head_rows[:, 0], preferred_element_type=jnp.float32)
    second_part = jnp.dot(hidden[1], head_rows[:, 1], preferred_element_type=jnp.float32)
    value_part = jnp.dot(hidden[2], head_rows[:, 2], preferred_element_type=jnp.float32)
    mean_part = jnp.dot(hidden[3], head_rows[:, 3:], preferred_element_type=jnp.float32)
    return (first_part, second_part, value_part, mean_part)


def shards(
    states,
    actions,
    rewards,
    terminal,
    next_index,
    hidden_weights,
    action_weights,
    heads,
    policy_scale,
):
    rows_here = states.shape[0]
    row_count = lax.axis_size("row")
    col_count = lax.axis_size("col")
    col_at = lax.axis_index("col")
    col_units = D // col_count
    total_rows = rows_here * lax.axis_size("dp") * row_count
    terms = jnp.einsum(
        "bk,nko->nbo",
        states,
        lax.all_gather(hidden_weights, "row", axis=2, tiled=True),
        preferred_element_type=jnp.float32,
    )
    summed = lax.psum_scatter(terms, "col", scatter_dimension=2, tiled=True)
    act_cols = lax.dynamic_slice_in_dim(action_weights, col_at * col_units, col_units, 2)
    extra = jnp.einsum("ba,nau->nbu", actions, act_cols, preferred_element_type=jnp.float32)
    pre = jnp.concatenate([summed[:2] + extra, summed[2:]], axis=0)
    hidden = jnp.maximum(pre, 0.0).astype(jnp.bfloat16)
    head_rows = lax.dynamic_slice_in_dim(heads, col_at * col_units, col_units, 0)
    parts = head_parts(hidden, head_rows)
    first_q, second_q, value, policy_mean = packed_total(
        (parts[0], parts[1], parts[2], parts[3]), "col"
    )
    advantage = jnp.minimum(first_q, second_q) - value
    value_whole = collect(value, ("dp", "row"), 0)
    top = over_copies(jnp.max(advantage), ("dp", "row"))
    target = rewards + GAMMA * (1.0 - terminal.astype(jnp.float32)) * jnp.take(
        value_whole, next_index, axis=0
    )
    weight = jnp.maximum(jnp.exp(advantage - top), FLOOR)
    expectile = jnp.where(advantage >= 0.0, TAU, 1.0 - TAU)
    scaled = (actions.astype(jnp.float32) - policy_mean) / policy_scale
    log_prob = -0.5 * jnp.sum(scaled * scaled, axis=1)
    value_terms = expectile * advantage * advantage
    critic_terms = (first_q - target) ** 2 + (second_q - target) ** 2
    policy_terms = -weight * log_prob
    coeff_first = (2.0 * (first_q - target))[:, None]
    coeff_second = (2.0 * (second_q - target))[:, None]
    coeff_value = (-2.0 * expectile * advantage)[:, None]
    coeff_policy = -weight[:, None] * scaled / policy_scale
    loss_terms = jnp.stack([jnp.sum(value_terms), jnp.sum(critic_terms), jnp.sum(policy_terms)])
    columns = [
        (hidden[0], coeff_first),
        (hidden[1], coeff_second),
        (hidden[2], coeff_value),
        (hidden[3], coeff_policy),
    ]
    grad_local = jnp.concatenate(
        [
            jnp.dot(units.astype(jnp.float32).T, coeff, precision=lax.Precision.HIGHEST)
            for units, coeff in columns
        ],
        axis=1,
    )
    grad_sum, loss_sum = packed_total((grad_local, loss_terms), ("dp", "row"))
    grad_whole = collect(grad_sum, "col", 0)
    return (advantage, loss_sum / total_rows, grad_whole / math.sqrt(total_rows))


def solution(mesh):
    return jax.shard_map(
        shards,
        mesh=mesh,
        in_specs=(
            P(("dp", "row"), "col"),
            P(("dp", "row"), None),
            P(("dp", "row")),
            P(("dp", "row")),
            P(("dp", "row")),
            P(None, "col", "row"),
            P(),
            P(),
            P(),
        ),
        out_specs=(P(("dp", "row")), P(), P()),
        check_vma=False,
    )
```

profile of v0, /device:TPU:1, one launch (start us, length us, event | category | flops | bytes accessed | tf_op | source)
XLA Modules:
  0.0 523.0 jit_solution(15195396994888836502)
XLA Ops:
  7.2 2.3 copy.44
  9.6 121.0 %all-gather.2.cloned.1.call-done = bf16[4,512,4096]{1,2,0:T(8,128)(2,1)} async-done(((bf16[4,512,256]{1,2,0:T(8,128)(2,1)}), bf16[4,512,4096]{1,2,0:T(8,128)(2,1)}) %all-gather.2.cloned.1.call-update) | async-done | bytes 16777232 | tf_op jit(solution)/shard_map/all_gather | solution.py:74
  130.6 17.0 %convolution_bitcast_fusion = f32[4,384,4096]{1,2,0:T(8,128)} fusion(bf16[4,512,4096]{1,2,0:T(8,128)(2,1)} %all-gather.2.cloned.1.call-done, bf16[384,512]{1,0:T(8,128)(2,1)S(1)} %copy-done), kind=kOutput, calls=%fused_computation.1 | convolution fusion | flops 6442450944 | bytes 42336256 | tf_op jit(solution)/shard_map/bk,nko->nbo/dot_general | solution.py:71
  147.6 252.4 %reduce-scatter.2.cloned.1.call-done = f32[4,384,512]{1,2,0:T(8,128)} async-done(((f32[4,384,4096]{1,2,0:T(8,128)}), f32[4,384,512]{1,2,0:T(8,128)}) %reduce-scatter.2.cloned.1.call-update) | async-done | bytes 3145744 | tf_op jit(solution)/shard_map/reduce_scatter | solution.py:77
  400.0 1.5 slice.79
  401.6 1.8 slice_add_fusion
  404.6 1.1 fusion.4
  405.9 0.9 convolution_reduce_fusion
  406.8 0.9 convolution_reduce_fusion.1
  408.6 4.2 all-to-all-start
  412.9 12.2 %all-to-all-done = f32[8,1,10368]{2,1,0:T(1,128)S(1)} async-done(((f32[8,1,10368]{2,1,0:T(1,128)}), f32[8,1,10368]{2,1,0:T(1,128)S(1)}, u32[]{:S(2)}, u32[]{:S(2)}) %all-to-all-start) | async-done | bytes 331808 | tf_op jit(solution)/shard_map/all_to_all | solution.py:15
  426.0 9.0 %all-to-all-start.1 = ((f32[32,1,384]{2,1,0:T(1,128)}), f32[32,1,384]{2,1,0:T(1,128)S(1)}, u32[]{:S(2)}, u32[]{:S(2)}) async-start(f32[32,1,384]{2,1,0:T(1,128)} %broadcast_in_dim.38), calls=%async_computation.2 | async-start | bytes 98304 | tf_op jit(solution)/shard_map/all_to_all | solution.py:15
  435.3 6.7 %all-to-all-done.1 = f32[32,1,384]{2,1,0:T(1,128)S(1)} async-done(((f32[32,1,384]{2,1,0:T(1,128)}), f32[32,1,384]{2,1,0:T(1,128)S(1)}, u32[]{:S(2)}, u32[]{:S(2)}) %all-to-all-start.1) | async-done | bytes 49184 | tf_op jit(solution)/shard_map/all_to_all | solution.py:15
  442.0 2.5 gather_fusion
  445.9 1.2 broadcast_in_dim.43
  447.1 4.2 all-to-all-start.2
  452.5 5.5 %all-to-all-done.2 = f32[32,1,1]{2,1,0:T(1,128)S(1)} async-done(((f32[32,1,1]{2,1,0:T(1,128)}), f32[32,1,1]{2,1,0:T(1,128)S(1)}, u32[]{:S(2)}, u32[]{:S(2)}) %all-to-all-start.2) | async-done | bytes 160 | tf_op jit(solution)/shard_map/all_to_all | solution.py:15
  458.6 1.2 multiply_reduce_fusion.1
  460.7 2.0 concatenate.15
  463.6 28.2 %all_to_all.29 = f32[32,1,13827]{2,1,0:T(1,128)S(1)} all-to-all(f32[32,1,13827]{2,1,0:T(1,128)S(1)} %broadcast_in_dim.44), channel_id=1, replica_groups=mesh['dp'=2,'row'=16,'col'=8] {'dp','row'}, dimensions={0} | all-to-all | bytes 3539712 | tf_op jit(solution)/shard_map/all_to_all | solution.py:15
  491.9 1.0 reduce_sum.59
  494.1 3.5 all-to-all-start.4
  498.1 16.6 %all-to-all-done.4 = f32[8,512,27]{1,2,0:T(8,128)S(1)} async-done(((f32[8,512,27]{1,2,0:T(8,128)}), f32[8,512,27]{1,2,0:T(8,128)S(1)}, u32[]{:S(2)}, u32[]{:S(2)}) %all-to-all-start.4) | async-done | bytes 442400 | tf_op jit(solution)/shard_map/all_to_all | solution.py:15
  515.1 1.1 copy.63
  (53 shorter events, 10.6 us)
Async XLA Ops:
  7.2 123.4 %copy-start = (bf16[384,512]{1,0:T(8,128)(2,1)S(1)}, bf16[384,512]{1,0:T(8,128)(2,1)}, u32[]{:S(2)}) copy-start(bf16[384,512]{1,0:T(8,128)(2,1)} %param.9) | copy-start | bytes 1179652
  7.2 123.4 %all-gather.2.cloned.1.call-start = ((), (), s32[]{:S(2)}) async-start(), calls=%async_computation.6 | async-start | bytes 17825792 | tf_op jit(solution)/shard_map/all_gather | solution.py:74
  9.6 390.5 %reduce-scatter.2.cloned.1.call-start = ((), (), s32[]{:S(2)}) async-start(), calls=%async_computation.7 | async-start | bytes 28311552 | tf_op jit(solution)/shard_map/reduce_scatter | solution.py:77
  147.6 254.0 %copy-start.1 = (bf16[384,24]{0,1:T(8,128)(2,1)S(1)}, bf16[384,24]{0,1:T(8,128)(2,1)}, u32[]{:S(2)}) copy-start(bf16[384,24]{0,1:T(8,128)(2,1)} %param.10) | copy-start | bytes 55300
  404.6 8.3 %copy-start.3 = (s32[384]{0:T(512)S(1)}, s32[384]{0:T(512)}, u32[]{:S(2)}) copy-start(s32[384]{0:T(512)} %param.13) | copy-start | bytes 4612
  405.8 29.4 %copy-start.6 = (f32[24]{0:T(128)S(1)}, f32[24]{0:T(128)}, u32[]{:S(2)}) copy-start(f32[24]{0:T(128)} %param.17) | copy-start | bytes 292
  408.6 16.4 %all-to-all-start = ((f32[8,1,10368]{2,1,0:T(1,128)}), f32[8,1,10368]{2,1,0:T(1,128)S(1)}, u32[]{:S(2)}, u32[]{:S(2)}) async-start(f32[8,1,10368]{2,1,0:T(1,128)} %broadcast_in_dim.37), calls=%async_computation.1 | async-start | bytes 663552 | tf_op jit(solution)/shard_map/all_to_all | solution.py:15
  412.9 31.7 %copy-start.4 = (f32[384]{0:T(512)S(1)}, f32[384]{0:T(512)}, u32[]{:S(2)}) copy-start(f32[384]{0:T(512)} %param.11) | copy-start | bytes 4612
  412.9 31.7 %copy-start.5 = (s32[384]{0:T(512)S(1)}, s32[384]{0:T(512)}, u32[]{:S(2)}) copy-start(s32[384]{0:T(512)} %param.12) | copy-start | bytes 4612
  426.0 16.0 %all-to-all-start.1 = ((f32[32,1,384]{2,1,0:T(1,128)}), f32[32,1,384]{2,1,0:T(1,128)S(1)}, u32[]{:S(2)}, u32[]{:S(2)}) async-start(f32[32,1,384]{2,1,0:T(1,128)} %broadcast_in_dim.38), calls=%async_computation.2 | async-start | bytes 98304 | tf_op jit(solution)/shard_map/all_to_all | solution.py:15
  445.2 18.4 %copy-start.2 = (f32[384]{0:T(512)}, f32[384]{0:T(512)S(1)}, u32[]{:S(2)}) copy-start(f32[384]{0:T(512)S(1)} %get-tuple-element.14) | copy-start | bytes 4612
  447.1 11.0 %all-to-all-start.2 = ((f32[32,1,1]{2,1,0:T(1,128)}), f32[32,1,1]{2,1,0:T(1,128)S(1)}, u32[]{:S(2)}, u32[]{:S(2)}) async-start(f32[32,1,1]{2,1,0:T(1,128)} %broadcast_in_dim.43), calls=%async_computation.3 | async-start | bytes 32768 | tf_op jit(solution)/shard_map/all_to_all | solution.py:15
  494.1 20.6 %all-to-all-start.4 = ((f32[8,512,27]{1,2,0:T(8,128)}), f32[8,512,27]{1,2,0:T(8,128)S(1)}, u32[]{:S(2)}, u32[]{:S(2)}) async-start(f32[8,512,27]{1,2,0:T(8,128)} %broadcast_in_dim.45), calls=%async_computation.5 | async-start | bytes 1048576 | tf_op jit(solution)/shard_map/all_to_all | solution.py:15
Sparse Core Ops, SparseCore 0:
  10.5 120.0 all-gather.1
  147.7 252.2 reduce-scatter.1
where the time goes:
time: 524 us; the launch traced here: 523 us
  waiting for transfers between devices  414 us (79%)
  blocking collectives  28.2 us (5%)
  matrix products  24.3 us (5%)
  starting transfers between devices  21 us (4%)
  local copies, waits for them, and re-layouts  15.1 us (3%)
  between operations  14.3 us (3%)
  other arithmetic  5.71 us (1%)
    reduce_scatter x1, waiting for transfers between devices, shards(): summed = lax.psum_scatter(terms, 'col', scatter_dimension=2, tiled=True)  252 us
    all_gather x1, waiting for transfers between devices, shards(): lax.all_gather(hidden_weights, 'row', axis=2, tiled=True)  121 us
    all_to_all x4, waiting for transfers between devices, from_everyone(): return lax.all_to_all(copies, axis, split_axis=0, concat_axis=0, tiled=True)  40.9 us
    all_to_all x1, blocking collectives, from_everyone(): return lax.all_to_all(copies, axis, split_axis=0, concat_axis=0, tiled=True)  28.2 us
    all_to_all x4, starting transfers between devices, from_everyone(): return lax.all_to_all(copies, axis, split_axis=0, concat_axis=0, tiled=True)  20.9 us
    dot_general x1, matrix products, shards(): jnp.einsum('bk,nko->nbo', states, lax.all_gather(hidden_weights, 'row', a...  17 us
  transfers between devices with their start and end apart: 6, of which 6 were waited for; matrix products, arithmetic and copies ran while one was open for 0% of the time, Pallas kernels for 0%

commit v1 on v0

--- a/solution.py
+++ b/solution.py
@@ -71,7 +71,9 @@
     terms = jnp.einsum(
         "bk,nko->nbo",
         states,
-        lax.all_gather(hidden_weights, "row", axis=2, tiled=True),
+        jnp.concatenate(
+            lax.all_to_all(jnp.stack([hidden_weights] * lax.axis_size("row")), "row", 0, 0), axis=2
+        ),
         preferred_element_type=jnp.float32,
     )
     summed = lax.psum_scatter(terms, "col", scatter_dimension=2, tiled=True)

time: 524 us -> 603 us (1.15)
  blocking collectives: 28.2 us -> 220 us
  waiting for transfers between devices: 414 us -> 294 us
  local copies, waits for them, and re-layouts: 15.1 us -> 23.1 us
    all_to_all x0 -> x1, blocking collectives: none -> 192 us  [shards(): lax.all_to_all(jnp.stack([hidden_weights] * lax.axis_size('row')), 'row',...]
    all_gather x1 -> x0, waiting for transfers between devices: 121 us -> none  [shards(): lax.all_gather(hidden_weights, 'row', axis=2, tiled=True)]
    reshape x0 -> x1, local copies, waits for them, and re-layouts: none -> 7.05 us  [shards(): jnp.concatenate(lax.all_to_all(jnp.stack([hidden_weights] * lax.axis_size...]
  transfers between devices with their start and end apart: 6 -> 5, of which waited for: 6 -> 5; matrix products, arithmetic and copies ran while one was open for 0% -> 0% of each run, Pallas kernels for 0% -> 0%
where the time goes in v1:
time: 603 us
  waiting for transfers between devices  294 us (49%)
  blocking collectives  220 us (36%)
  matrix products  24.3 us (4%)
  local copies, waits for them, and re-layouts  23.1 us (4%)
  starting transfers between devices  21 us (3%)
  between operations  14.3 us (2%)
    reduce_scatter x1, waiting for transfers between devices, shards(): summed = lax.psum_scatter(terms, 'col', scatter_dimension=2, tiled=True)  253 us
    all_to_all x1, blocking collectives, shards(): lax.all_to_all(jnp.stack([hidden_weights] * lax.axis_size('row')), 'row',...  192 us
    all_to_all x4, waiting for transfers between devices, from_everyone(): return lax.all_to_all(copies, axis, split_axis=0, concat_axis=0, tiled=True)  40.8 us
    all_to_all x1, blocking collectives, from_everyone(): return lax.all_to_all(copies, axis, split_axis=0, concat_axis=0, tiled=True)  28.2 us
    all_to_all x4, starting transfers between devices, from_everyone(): return lax.all_to_all(copies, axis, split_axis=0, concat_axis=0, tiled=True)  20.9 us
    dot_general x1, matrix products, shards(): jnp.einsum('bk,nko->nbo', states, jnp.concatenate(lax.all_to_all(jnp.stac...  17 us
  transfers between devices with their start and end apart: 5, of which 5 were waited for; matrix products, arithmetic and copies ran while one was open for 0% of the time, Pallas kernels for 0%

profile of v1, /device:TPU:1, one launch (start us, length us, event | category | flops | bytes accessed | tf_op | source)
XLA Modules:
  0.0 602.6 jit_solution(15702464545975672642)
XLA Ops:
  7.2 1.5 copy.48
  8.8 1.7 stack.8
  10.5 192.0 %all_to_all.34 = bf16[16,4,512,256]{2,3,1,0:T(8,128)(2,1)S(1)} all-to-all(bf16[16,4,512,256]{2,3,1,0:T(8,128)(2,1)S(1)} %stack.8), channel_id=1, replica_groups=mesh['dp'=2,'row'=16,'col'=8] {'row'}, dimensions={0} | all-to-all | bytes 33554432 | tf_op jit(solution)/shard_map/all_to_all | solution.py:75
  202.6 7.1 %copy.49 = bf16[4,512,16,256]{1,3,2,0:T(8,128)(2,1)} copy(bf16[4,512,16,256]{1,3,0,2:T(8,128)(2,1)S(1)} %bitcast.53) | data formatting | bytes 33554432 | tf_op jit(solution)/shard_map/reshape | solution.py:74
  209.6 17.0 %convolution_bitcast_fusion = f32[4,384,4096]{1,2,0:T(8,128)} fusion(bf16[4,512,4096]{1,2,0:T(8,128)(2,1)} %bitcast.54, bf16[384,512]{1,0:T(8,128)(2,1)S(1)} %copy-done), kind=kOutput, calls=%fused_computation.1 | convolution fusion | flops 6442450944 | bytes 42336256 | tf_op jit(solution)/shard_map/bk,nko->nbo/dot_general | solution.py:71
  226.6 253.0 %reduce-scatter.2.cloned.1.call-done = f32[4,384,512]{1,2,0:T(8,128)} async-done(((f32[4,384,4096]{1,2,0:T(8,128)}), f32[4,384,512]{1,2,0:T(8,128)}) %reduce-scatter.2.cloned.1.call-update) | async-done | bytes 3145744 | tf_op jit(solution)/shard_map/reduce_scatter | solution.py:79
  479.7 1.5 slice.79
  481.2 1.8 slice_add_fusion
  484.2 1.1 fusion.4
  488.3 4.2 all-to-all-start.1
  492.5 12.1 %all-to-all-done.1 = f32[8,1,10368]{2,1,0:T(1,128)S(1)} async-done(((f32[8,1,10368]{2,1,0:T(1,128)}), f32[8,1,10368]{2,1,0:T(1,128)S(1)}, u32[]{:S(2)}, u32[]{:S(2)}) %all-to-all-start.1) | async-done | bytes 331808 | tf_op jit(solution)/shard_map/all_to_all | solution.py:15
  505.6 9.0 %all-to-all-start.2 = ((f32[32,1,384]{2,1,0:T(1,128)}), f32[32,1,384]{2,1,0:T(1,128)S(1)}, u32[]{:S(2)}, u32[]{:S(2)}) async-start(f32[32,1,384]{2,1,0:T(1,128)} %broadcast_in_dim.38), calls=%async_computation.3 | async-start | bytes 98304 | tf_op jit(solution)/shard_map/all_to_all | solution.py:15
  514.9 6.7 %all-to-all-done.2 = f32[32,1,384]{2,1,0:T(1,128)S(1)} async-done(((f32[32,1,384]{2,1,0:T(1,128)}), f32[32,1,384]{2,1,0:T(1,128)S(1)}, u32[]{:S(2)}, u32[]{:S(2)}) %all-to-all-start.2) | async-done | bytes 49184 | tf_op jit(solution)/shard_map/all_to_all | solution.py:15
  521.6 2.5 gather_fusion
  525.5 1.2 broadcast_in_dim.43
  526.7 4.2 all-to-all-start.3
  532.1 5.5 all-to-all-done.3
  538.3 1.2 multiply_reduce_fusion.1
  540.3 2.0 concatenate.15
  543.2 28.2 %all_to_all.35 = f32[32,1,13827]{2,1,0:T(1,128)S(1)} all-to-all(f32[32,1,13827]{2,1,0:T(1,128)S(1)} %broadcast_in_dim.44), channel_id=1, replica_groups=mesh['dp'=2,'row'=16,'col'=8] {'dp','row'}, dimensions={0} | all-to-all | bytes 3539712 | tf_op jit(solution)/shard_map/all_to_all | solution.py:15
  571.5 1.0 reduce_sum.59
  573.7 3.5 all-to-all-start.5
  577.8 16.6 %all-to-all-done.5 = f32[8,512,27]{1,2,0:T(8,128)S(1)} async-done(((f32[8,512,27]{1,2,0:T(8,128)}), f32[8,512,27]{1,2,0:T(8,128)S(1)}, u32[]{:S(2)}, u32[]{:S(2)}) %all-to-all-start.5) | async-done | bytes 442400 | tf_op jit(solution)/shard_map/all_to_all | solution.py:15
  594.7 1.1 copy.68
  (55 shorter events, 12.4 us)
Async XLA Ops:
  7.2 202.4 %copy-start = (bf16[384,512]{1,0:T(8,128)(2,1)S(1)}, bf16[384,512]{1,0:T(8,128)(2,1)}, u32[]{:S(2)}) copy-start(bf16[384,512]{1,0:T(8,128)(2,1)} %param.9) | copy-start | bytes 1179652
  7.2 472.5 %reduce-scatter.2.cloned.1.call-start = ((), (), s32[]{:S(2)}) async-start(), calls=%async_computation.7 | async-start | bytes 28311552 | tf_op jit(solution)/shard_map/reduce_scatter | solution.py:79
  226.6 254.6 %copy-start.2 = (bf16[384,24]{0,1:T(8,128)(2,1)S(1)}, bf16[384,24]{0,1:T(8,128)(2,1)}, u32[]{:S(2)}) copy-start(bf16[384,24]{0,1:T(8,128)(2,1)} %param.10) | copy-start | bytes 55300
  484.2 8.3 %copy-start.4 = (s32[384]{0:T(512)S(1)}, s32[384]{0:T(512)}, u32[]{:S(2)}) copy-start(s32[384]{0:T(512)} %param.13) | copy-start | bytes 4612
  485.5 29.4 %copy-start.7 = (f32[24]{0:T(128)S(1)}, f32[24]{0:T(128)}, u32[]{:S(2)}) copy-start(f32[24]{0:T(128)} %param.17) | copy-start | bytes 292
  488.3 16.4 %all-to-all-start.1 = ((f32[8,1,10368]{2,1,0:T(1,128)}), f32[8,1,10368]{2,1,0:T(1,128)S(1)}, u32[]{:S(2)}, u32[]{:S(2)}) async-start(f32[8,1,10368]{2,1,0:T(1,128)} %broadcast_in_dim.37), calls=%async_computation.2 | async-start | bytes 663552 | tf_op jit(solution)/shard_map/all_to_all | solution.py:15
  492.5 31.7 %copy-start.5 = (f32[384]{0:T(512)S(1)}, f32[384]{0:T(512)}, u32[]{:S(2)}) copy-start(f32[384]{0:T(512)} %param.11) | copy-start | bytes 4612
  492.5 31.7 %copy-start.6 = (s32[384]{0:T(512)S(1)}, s32[384]{0:T(512)}, u32[]{:S(2)}) copy-start(s32[384]{0:T(512)} %param.12) | copy-start | bytes 4612
  505.6 16.1 %all-to-all-start.2 = ((f32[32,1,384]{2,1,0:T(1,128)}), f32[32,1,384]{2,1,0:T(1,128)S(1)}, u32[]{:S(2)}, u32[]{:S(2)}) async-start(f32[32,1,384]{2,1,0:T(1,128)} %broadcast_in_dim.38), calls=%async_computation.3 | async-start | bytes 98304 | tf_op jit(solution)/shard_map/all_to_all | solution.py:15
  524.8 18.4 %copy-start.3 = (f32[384]{0:T(512)}, f32[384]{0:T(512)S(1)}, u32[]{:S(2)}) copy-start(f32[384]{0:T(512)S(1)} %get-tuple-element.14) | copy-start | bytes 4612
  526.7 11.0 %all-to-all-start.3 = ((f32[32,1,1]{2,1,0:T(1,128)}), f32[32,1,1]{2,1,0:T(1,128)S(1)}, u32[]{:S(2)}, u32[]{:S(2)}) async-start(f32[32,1,1]{2,1,0:T(1,128)} %broadcast_in_dim.43), calls=%async_computation.4 | async-start | bytes 32768 | tf_op jit(solution)/shard_map/all_to_all | solution.py:15
  573.7 20.6 %all-to-all-start.5 = ((f32[8,512,27]{1,2,0:T(8,128)}), f32[8,512,27]{1,2,0:T(8,128)S(1)}, u32[]{:S(2)}, u32[]{:S(2)}) async-start(f32[8,512,27]{1,2,0:T(8,128)} %broadcast_in_dim.45), calls=%async_computation.6 | async-start | bytes 1048576 | tf_op jit(solution)/shard_map/all_to_all | solution.py:15
  577.2 18.5 %copy-start.1 = (bf16[384,512]{1,0:T(8,128)(2,1)S(1)}, bf16[384,512]{1,0:T(8,128)(2,1)}, u32[]{:S(2)}) copy-start(bf16[384,512]{1,0:T(8,128)(2,1)} %param.9) | copy-start | bytes 1179652
Sparse Core Ops, SparseCore 0:
  226.7 252.8 reduce-scatter.1
